TPU v7x, 32 devices: a whole 2x2x4 slice. The times are simulated.
32 devices in a mesh: scan: 16 (over z, x, core), dict: 2 (over y).
Axes of the slice: x: 2, y: 2, z: 4, core: 2. Of those that a mesh axis runs over, the one named last changes fastest.
Arguments:
- patterns: bfloat16 [3600, 16384], P(None, 'scan'), may hold values from -210 to 210
- dictionary: bfloat16 [3600, 8192], P(None, ('scan', 'dict')), may hold values from -70 to 70
- orientation_quats: bfloat16 [4, 8192], P(None, ('scan', 'dict')), may hold values from -1 to 1
- phase_id: int32 [8192], P(('scan', 'dict')), may hold values from 0 to 2, as said below
- valid_count: int32 [32], P(('scan', 'dict')), may hold values from 1 to 256
Outputs:
- mean_quat: float32 [4, 16384], P(None, 'scan')
- phase_prob: float32 [3, 16384], P(None, 'scan')
Inputs may be any that keep to these rules, and one draw needn't show every extreme that they name: `phase_id`: constant within each tile of 256 slots.
All inputs are finite; a program needn't handle non-finite values.
Results may differ from a plain program's by a relative error of at most 0.0029.
Values may be sent and summed in bfloat16 or wider, within the bound.
A program may use at most 128 MiB of HBM per device.

v0:
```python
import jax
import jax.numpy as jnp
from jax import lax
from jax.sharding import PartitionSpec as P

REACH = 3


EPS = 1e-05
SHARPNESS = 40.0


def from_behind(block, axis, distance):
    devices = range(lax.axis_size(axis))
    route = [((i - distance) % len(devices), i) for i in devices]
    return lax.ppermute(block, axis, route)


def unit_columns(values):
    widened = values.astype(jnp.float32)
    centred = widened - jnp.mean(widened, axis=0, keepdims=True)
    mean_square = jnp.mean(centred * centred, axis=0, keepdims=True)
    return (centred * lax.rsqrt((mean_square + EPS) * values.shape[0])).astype(jnp.bfloat16)


def contribute(unit_tile, table_rows, unit_pats):
    cosine = lax.dot_general(
        unit_tile, unit_pats, (((0,), (0,)), ((), ())), preferred_element_type=jnp.float32
    )
    weights = jnp.exp(SHARPNESS * (cosine - 1.0)).astype(jnp.bfloat16)
    return jnp.dot(table_rows, weights, preferred_element_type=jnp.float32)


def per_device(patterns, dictionary, orientation_quats, phase_id, valid_count):
    pixels = dictionary.shape[0]
    tile_size = dictionary.shape[1]
    live_slots = (jnp.arange(tile_size) < valid_count[0]).astype(jnp.float32)
    phase_rows = (phase_id[None, :] == jnp.arange(3)[:, None]).astype(jnp.float32)
    tile_table = jnp.concatenate(
        [orientation_quats.astype(jnp.float32), phase_rows, jnp.ones((1, tile_size), jnp.float32)],
        0,
    )
    tile_table = (tile_table * live_slots[None, :]).astype(jnp.bfloat16)
    packed = jnp.concatenate([unit_columns(dictionary), tile_table], 0)
    unit_pats = unit_columns(patterns)

    def absorb_tile(running, packed_tile):
        unit_tile = packed_tile[:pixels]
        table_rows = packed_tile[pixels:]
        return running + contribute(unit_tile, table_rows, unit_pats)

    running = absorb_tile(jnp.zeros((8, patterns.shape[1]), jnp.float32), packed)
    from_lower = packed
    from_upper = packed
    for hop_index in range(REACH):
        from_lower = from_behind(from_lower, "scan", 1)
        from_upper = from_behind(from_upper, "scan", -1)
        running = absorb_tile(absorb_tile(running, from_lower), from_upper)
    totals = lax.psum(running, "dict")
    denominator = totals[7:8]
    return (totals[0:4] / denominator, totals[4:7] / denominator)


def solution(mesh):
    in_specs = (
        P(None, "scan"),
        P(None, ("scan", "dict")),
        P(None, ("scan", "dict")),
        P(("scan", "dict")),
        P(("scan", "dict")),
    )
    out_specs = (P(None, "scan"), P(None, "scan"))
    return jax.shard_map(
        per_device, mesh=mesh, in_specs=in_specs, out_specs=out_specs, check_vma=False
    )
```

profile of v0, /device:TPU:1, one launch (start us, length us, event | category | flops | bytes accessed | tf_op | source)
XLA Modules:
  0.0 156.8 jit_solution(6198188156101191845)
XLA Ops:
  0.6 0.0 copy-start.1
  0.6 0.0 copy-start
  0.7 2.1 %convert_reduce_fusion.1 = f32[256]{0:T(256)S(1)} fusion(bf16[3600,256]{1,0:T(8,128)(2,1)} %param.6), kind=kLoop, calls=%fused_computation.7 | loop fusion | flops 1842944 | bytes 1844224 | tf_op jit(solution)/shard_map/reduce_sum | solution.py:21
  2.8 2.5 %fusion.6 = f32[256]{0:T(256)S(1)} fusion(bf16[3600,256]{1,0:T(8,128)(2,1)} %param.6, f32[256]{0:T(256)S(1)} %broadcast_multiply_fusion.1), kind=kLoop, calls=%fused_computation.10 | loop fusion | flops 3686144 | bytes 1845248 | tf_op jit(solution)/shard_map/reduce_sum | solution.py:22
  5.3 2.0 %fusion.7 = bf16[3600,256]{1,0:T(8,128)(2,1)S(1)} fusion(bf16[3600,256]{1,0:T(8,128)(2,1)} %param.6, f32[256]{0:T(256)S(1)} %multiply_rsqrt_fusion.1, f32[256]{0:T(256)S(1)} %broadcast_multiply_fusion.1), kind=kLoop, calls=%fused_computation.11 | loop fusion | flops 3686400 | bytes 3688448 | tf_op jit(solution)/shard_map/convert_element_type | solution.py:23
  8.0 0.1 pad.4.clone
  8.1 0.1 fusion.146
  8.1 0.1 pad_maximum_fusion
  8.3 0.1 collective-permute-start.1
  8.4 2.6 %collective-permute-start = (bf16[3608,256]{1,0:T(8,128)(2,1)S(1)}, bf16[3608,256]{1,0:T(8,128)(2,1)}, u32[]{:S(2)}, u32[]{:S(2)}) collective-permute-start(bf16[3608,256]{1,0:T(8,128)(2,1)S(1)} %pad_maximum_fusion), channel_id=1, source_target_pairs={{30,0},{0,2},{2,4},{4,6},{6,8},{8,10},{10,12},{12,14},{14,16},{16,... | collective-permute-start | bytes 5541896 | tf_op jit(solution)/shard_map/ppermute | solution.py:16
  11.0 1.1 convert_reduce_fusion
  12.1 2.0 %fusion.2 = f32[1024]{0:T(1024)S(1)} fusion(bf16[3600,1024]{1,0:T(8,128)(2,1)S(1)} %copy-done, f32[1024]{0:T(1024)S(1)} %broadcast_multiply_fusion), kind=kLoop, calls=%fused_computation.4 | loop fusion | flops 14744576 | bytes 7380992 | tf_op jit(solution)/shard_map/reduce_sum | solution.py:22
  14.1 37.8 %collective-permute-done.1 = bf16[3608,256]{1,0:T(8,128)(2,1)} collective-permute-done((bf16[3608,256]{1,0:T(8,128)(2,1)S(1)}, bf16[3608,256]{1,0:T(8,128)(2,1)}, u32[]{:S(2)}, u32[]{:S(2)}) %collective-permute-start.1) | collective-permute-done | bytes 1847328 | tf_op jit(solution)/shard_map/ppermute | solution.py:16
  51.8 0.0 collective-permute-start.3
  51.9 19.0 %collective-permute-done = bf16[3608,256]{1,0:T(8,128)(2,1)} collective-permute-done((bf16[3608,256]{1,0:T(8,128)(2,1)S(1)}, bf16[3608,256]{1,0:T(8,128)(2,1)}, u32[]{:S(2)}, u32[]{:S(2)}) %collective-permute-start) | collective-permute-done | bytes 1847328 | tf_op jit(solution)/shard_map/ppermute | solution.py:16
  70.9 2.6 %collective-permute-start.2 = (bf16[3608,256]{1,0:T(8,128)(2,1)}, bf16[3608,256]{1,0:T(8,128)(2,1)}, u32[]{:S(2)}, u32[]{:S(2)}) collective-permute-start(bf16[3608,256]{1,0:T(8,128)(2,1)} %collective-permute-done), channel_id=1, source_target_pairs={{30,0},{0,2},{2,4},{4,6},{6,8},{8,10},{10,12},{12,14},{14,16},{16,... | collective-permute-start | bytes 5541896 | tf_op jit(solution)/shard_map/ppermute | solution.py:16
  73.4 5.6 %fusion.113 = f32[8,1024]{1,0:T(8,128)S(1)} fusion(bf16[8,256]{1,0:T(8,128)(2,1)S(1)} %fusion.146, bf16[3600,256]{1,0:T(8,128)(2,1)S(1)} %fusion.7, bf16[3600,1024]{1,0:T(8,128)(2,1)} %param.5, f32[1024]{0:T(1024)S(1)} %multiply_rsqrt_fusion, f32[1024]{0:T(1024)S(1)} %broadcast_multiply_fusion), kind=kOutput, calls=%fused_computation.59 | convolution fusion | flops 1907163136 | bytes 9261056 | tf_op jit(solution)/shard_map/dot_general | solution.py:31
  79.0 6.1 %fusion.129 = f32[8,1024]{1,0:T(8,128)S(1)} fusion(f32[8,1024]{1,0:T(8,128)S(1)} %fusion.113, bf16[3608,256]{1,0:T(8,128)(2,1)} %collective-permute-done, bf16[3600,1024]{1,0:T(8,128)(2,1)} %param.5, f32[1024]{0:T(1024)S(1)} %multiply_rsqrt_fusion, f32[1024]{0:T(1024)S(1)} %broadcast_multiply_fusion), kind=kOutput, calls=%fused_computation.65 | convolution fusion | flops 1907171328 | bytes 9293824 | tf_op jit(solution)/shard_map/dot_general | solution.py:31
  85.1 9.6 %collective-permute-done.3 = bf16[3608,256]{1,0:T(8,128)(2,1)} collective-permute-done((bf16[3608,256]{1,0:T(8,128)(2,1)}, bf16[3608,256]{1,0:T(8,128)(2,1)}, u32[]{:S(2)}, u32[]{:S(2)}) %collective-permute-start.3) | collective-permute-done | bytes 1847328 | tf_op jit(solution)/shard_map/ppermute | solution.py:16
  94.7 0.0 collective-permute-start.5
  94.7 6.1 %fusion.126 = f32[8,1024]{1,0:T(8,128)S(1)} fusion(f32[8,1024]{1,0:T(8,128)S(1)} %fusion.129, bf16[3608,256]{1,0:T(8,128)(2,1)} %collective-permute-done.1, bf16[3600,1024]{1,0:T(8,128)(2,1)} %param.5, f32[1024]{0:T(1024)S(1)} %multiply_rsqrt_fusion, f32[1024]{0:T(1024)S(1)} %broadcast_multiply_fusion), kind=kOutput, calls=%fused_computation.64 | convolution fusion | flops 1907171328 | bytes 9293824 | tf_op jit(solution)/shard_map/dot_general | solution.py:31
  100.9 13.0 %collective-permute-done.2 = bf16[3608,256]{1,0:T(8,128)(2,1)} collective-permute-done((bf16[3608,256]{1,0:T(8,128)(2,1)}, bf16[3608,256]{1,0:T(8,128)(2,1)}, u32[]{:S(2)}, u32[]{:S(2)}) %collective-permute-start.2) | collective-permute-done | bytes 1847328 | tf_op jit(solution)/shard_map/ppermute | solution.py:16
  113.9 2.5 %collective-permute-start.4 = (bf16[3608,256]{1,0:T(8,128)(2,1)}, bf16[3608,256]{1,0:T(8,128)(2,1)}, u32[]{:S(2)}, u32[]{:S(2)}) collective-permute-start(bf16[3608,256]{1,0:T(8,128)(2,1)} %collective-permute-done.2), channel_id=1, source_target_pairs={{30,0},{0,2},{2,4},{4,6},{6,8},{8,10},{10,12},{12,14},{14,16},{16,... | collective-permute-start | bytes 5541896 | tf_op jit(solution)/shard_map/ppermute | solution.py:16
  116.3 6.1 %fusion.105 = f32[8,1024]{1,0:T(8,128)S(1)} fusion(bf16[3608,256]{1,0:T(8,128)(2,1)} %collective-permute-done.3, bf16[3600,1024]{1,0:T(8,128)(2,1)} %param.5, f32[1024]{0:T(1024)S(1)} %multiply_rsqrt_fusion, f32[1024]{0:T(1024)S(1)} %broadcast_multiply_fusion), kind=kOutput, calls=%fused_computation.56 | convolution fusion | flops 1907163136 | bytes 9261056 | tf_op jit(solution)/shard_map/dot_general | solution.py:31
  122.5 6.1 %fusion.123 = f32[8,1024]{1,0:T(8,128)S(1)} fusion(f32[8,1024]{1,0:T(8,128)S(1)} %fusion.105, f32[8,1024]{1,0:T(8,128)S(1)} %fusion.126, bf16[3608,256]{1,0:T(8,128)(2,1)} %collective-permute-done.2, bf16[3600,1024]{1,0:T(8,128)(2,1)} %param.5, f32[1024]{0:T(1024)S(1)} %multiply_rsqrt_fusion, f32[1024]{0:T(1024)S(1)} %broadcast_multiply_fusion), kind=kOutput, calls=%fused_computation.63 | convolution fusion | flops 1907179520 | bytes 9326592 | tf_op jit(solution)/shard_map/dot_general | solution.py:31
  128.6 9.0 %collective-permute-done.5 = bf16[3608,256]{1,0:T(8,128)(2,1)S(1)} collective-permute-done((bf16[3608,256]{1,0:T(8,128)(2,1)}, bf16[3608,256]{1,0:T(8,128)(2,1)S(1)}, u32[]{:S(2)}, u32[]{:S(2)}) %collective-permute-start.5) | collective-permute-done | bytes 1847328 | tf_op jit(solution)/shard_map/ppermute | solution.py:16
  137.5 5.6 %fusion.111 = f32[8,1024]{1,0:T(8,128)S(1)} fusion(bf16[3608,256]{1,0:T(8,128)(2,1)S(1)} %collective-permute-done.5, bf16[3600,1024]{1,0:T(8,128)(2,1)} %param.5, f32[1024]{0:T(1024)S(1)} %multiply_rsqrt_fusion, f32[1024]{0:T(1024)S(1)} %broadcast_multiply_fusion), kind=kOutput, calls=%fused_computation.58 | convolution fusion | flops 1907163136 | bytes 9261056 | tf_op jit(solution)/shard_map/dot_general | solution.py:31
  143.1 0.0 collective-permute-done.4
  143.1 6.1 %fusion.117 = f32[8,1024]{1,0:T(8,128)S(1)} fusion(f32[8,1024]{1,0:T(8,128)S(1)} %fusion.111, f32[8,1024]{1,0:T(8,128)S(1)} %fusion.123, bf16[3608,256]{1,0:T(8,128)(2,1)} %collective-permute-done.4, bf16[3600,1024]{1,0:T(8,128)(2,1)} %param.5, f32[1024]{0:T(1024)S(1)} %multiply_rsqrt_fusion, f32[1024]{0:T(1024)S(1)} %broadcast_multiply_fusion), kind=kOutput, calls=%fused_computation.61 | convolution fusion | flops 1907179520 | bytes 9326592 | tf_op jit(solution)/shard_map/dot_general | solution.py:31
  149.2 6.4 %psum.7 = f32[8,1024]{1,0:T(8,128)S(1)} all-reduce(f32[8,1024]{1,0:T(8,128)S(1)} %fusion.117), channel_id=1, replica_groups=mesh['scan'=16,'dict'=2] {'dict'}, use_global_device_ids=true, to_apply=%region_4.0 | all-reduce | flops 8192 | bytes 65536 | tf_op jit(solution)/shard_map/psum | solution.py:59
  155.6 0.6 slice_divide_fusion
  156.2 0.6 slice_divide_fusion.1
  (12 shorter events, 0.1 us)
Async XLA Ops:
  0.6 6.6 %copy-start.1 = (bf16[4,256]{1,0:T(4,128)(2,1)S(1)}, bf16[4,256]{1,0:T(4,128)(2,1)}, u32[]{:S(2)}) copy-start(bf16[4,256]{1,0:T(4,128)(2,1)} %param.7) | copy-start | bytes 6148
  0.6 6.7 %copy-start.2 = (s32[256]{0:T(256)S(1)}, s32[256]{0:T(256)}, u32[]{:S(2)}) copy-start(s32[256]{0:T(256)} %param.8) | copy-start | bytes 3076
  0.6 10.3 %copy-start = (bf16[3600,1024]{1,0:T(8,128)(2,1)S(1)}, bf16[3600,1024]{1,0:T(8,128)(2,1)}, u32[]{:S(2)}) copy-start(bf16[3600,1024]{1,0:T(8,128)(2,1)} %param.5) | copy-start | bytes 22118404
  8.3 43.6 %collective-permute-start.1 = (bf16[3608,256]{1,0:T(8,128)(2,1)S(1)}, bf16[3608,256]{1,0:T(8,128)(2,1)}, u32[]{:S(2)}, u32[]{:S(2)}) collective-permute-start(bf16[3608,256]{1,0:T(8,128)(2,1)S(1)} %pad_maximum_fusion), channel_id=1, source_target_pairs={{2,0},{4,2},{6,4},{8,6},{10,8},{12,10},{14,12},{16,14},{18,16},{20... | collective-permute-start | bytes 5541896 | tf_op jit(solution)/shard_map/ppermute | solution.py:16
  8.4 62.5 %collective-permute-start = (bf16[3608,256]{1,0:T(8,128)(2,1)S(1)}, bf16[3608,256]{1,0:T(8,128)(2,1)}, u32[]{:S(2)}, u32[]{:S(2)}) collective-permute-start(bf16[3608,256]{1,0:T(8,128)(2,1)S(1)} %pad_maximum_fusion), channel_id=1, source_target_pairs={{30,0},{0,2},{2,4},{4,6},{6,8},{8,10},{10,12},{12,14},{14,16},{16,... | collective-permute-start | bytes 5541896 | tf_op jit(solution)/shard_map/ppermute | solution.py:16
  51.8 42.9 %collective-permute-start.3 = (bf16[3608,256]{1,0:T(8,128)(2,1)}, bf16[3608,256]{1,0:T(8,128)(2,1)}, u32[]{:S(2)}, u32[]{:S(2)}) collective-permute-start(bf16[3608,256]{1,0:T(8,128)(2,1)} %collective-permute-done.1), channel_id=1, source_target_pairs={{2,0},{4,2},{6,4},{8,6},{10,8},{12,10},{14,12},{16,14},{18,16},{20... | collective-permute-start | bytes 5541896 | tf_op jit(solution)/shard_map/ppermute | solution.py:16
  70.9 43.0 %collective-permute-start.2 = (bf16[3608,256]{1,0:T(8,128)(2,1)}, bf16[3608,256]{1,0:T(8,128)(2,1)}, u32[]{:S(2)}, u32[]{:S(2)}) collective-permute-start(bf16[3608,256]{1,0:T(8,128)(2,1)} %collective-permute-done), channel_id=1, source_target_pairs={{30,0},{0,2},{2,4},{4,6},{6,8},{8,10},{10,12},{12,14},{14,16},{16,... | collective-permute-start | bytes 5541896 | tf_op jit(solution)/shard_map/ppermute | solution.py:16
  94.7 42.8 %collective-permute-start.5 = (bf16[3608,256]{1,0:T(8,128)(2,1)}, bf16[3608,256]{1,0:T(8,128)(2,1)S(1)}, u32[]{:S(2)}, u32[]{:S(2)}) collective-permute-start(bf16[3608,256]{1,0:T(8,128)(2,1)} %collective-permute-done.3), channel_id=1, source_target_pairs={{2,0},{4,2},{6,4},{8,6},{10,8},{12,10},{14,12},{16,14},{18,16},{20... | collective-permute-start | bytes 5541896 | tf_op jit(solution)/shard_map/ppermute | solution.py:16
  113.9 29.2 %collective-permute-start.4 = (bf16[3608,256]{1,0:T(8,128)(2,1)}, bf16[3608,256]{1,0:T(8,128)(2,1)}, u32[]{:S(2)}, u32[]{:S(2)}) collective-permute-start(bf16[3608,256]{1,0:T(8,128)(2,1)} %collective-permute-done.2), channel_id=1, source_target_pairs={{30,0},{0,2},{2,4},{4,6},{6,8},{8,10},{10,12},{12,14},{14,16},{16,... | collective-permute-start | bytes 5541896 | tf_op jit(solution)/shard_map/ppermute | solution.py:16
where the time goes:
time: 157 us
  waiting for transfers between devices  88.4 us (56%)
  matrix products  41.7 us (27%)
  other arithmetic  11.1 us (7%)
  starting transfers between devices  7.79 us (5%)
  blocking collectives  6.35 us (4%)
    ppermute x6, waiting for transfers between devices, from_behind(): return lax.ppermute(block, axis, route)  88.4 us
    dot_general x7, matrix products, contribute(): return jnp.dot(table_rows, weights, preferred_element_type=jnp.float32)  41.7 us
    ppermute x6, starting transfers between devices, from_behind(): return lax.ppermute(block, axis, route)  7.79 us
    psum x1, blocking collectives, per_device(): totals = lax.psum(running, 'dict')  6.35 us
    reduce_sum x2, other arithmetic, unit_columns(): mean_square = jnp.mean(centred * centred, axis=0, keepdims=True)  4.47 us
    reduce_sum x2, other arithmetic, unit_columns(): centred = widened - jnp.mean(widened, axis=0, keepdims=True)  3.24 us
  transfers between devices with their start and end apart: 6, of which 5 were waited for; matrix products, arithmetic and copies ran while one was open for 25% of the time, Pallas kernels for 0%

commit v1 on v0

v1 whole, which is shorter than its diff:
```python
import functools

import jax
import jax.numpy as jnp
from jax import lax
from jax.experimental import pallas as pl
from jax.experimental.pallas import tpu as pltpu
from jax.sharding import PartitionSpec as P

REACH = 3
SLOTS = 2 * REACH + 1
EPS = 1e-05
SHARPNESS = 40.0
LAYER = 4


def chunk_count(pixels):
    for count in (5, 9, 3, 15, 2, 4, 8):
        if pixels % (16 * count) == 0:
            return count
    return 1


def kernel(
    n, n_dict, chunks, tile_ref, pats_ref, quats_ref, phase_ref, valid_ref,
    quat_out, prob_out,
    buf, pats, meta, acc, sums, totals,
    ssem, rsem, meta_ssem, meta_rsem, load_sem, sum_ssem, sum_rsem,
):
    pixels, slots = tile_ref.shape
    rows = pixels // chunks
    own = REACH
    me = lax.axis_index("scan")
    my_dict = lax.axis_index("dict")
    j = lax.rem(me, LAYER)
    sign = jnp.where(j < 2, 1, -1)
    role = jnp.where((j == 0) | (j == LAYER - 1), 0, 1)
    rho = 1 - 2 * role

    def at(offset):
        return lax.rem(me + offset + n, n)

    def chunk(i):
        return pl.ds(pl.multiple_of(i * rows, 16), rows)

    barrier = pltpu.get_barrier_semaphore()
    for offset in (-4, -3, -2, -1, 1, 2, 3, 4):
        pl.semaphore_signal(barrier, inc=1, device_id={"scan": at(offset)})
    for d in range(1, n_dict):
        pl.semaphore_signal(
            barrier, inc=1, device_id={"dict": lax.rem(my_dict + d, n_dict)}
        )
    load_pats = pltpu.make_async_copy(pats_ref, pats, load_sem.at[0])
    load_tile = pltpu.make_async_copy(tile_ref, buf.at[own], load_sem.at[1])
    load_tile.start()
    load_pats.start()
    pl.semaphore_wait(barrier, 8 + n_dict - 1)

    partner = rho * sign
    core_own = (0, None, partner, -rho)
    x_own = (1, None, 2 * sign, 2)
    z_own = (2, None, -3 * partner, 3 * rho)
    relay = (3, 2 + role, (4 - 2 * role) * sign, role - 2)
    core_mid = (4, 2, partner, 2 - rho)
    core_far = (5, -2, partner, -3)
    core_near = (6, -1, partner, -2)

    def send(flow, i):
        number, source, offset, slot = flow
        src = tile_ref.at[chunk(i)] if source is None else buf.at[source + own, chunk(i)]
        return pltpu.make_async_remote_copy(
            src_ref=src,
            dst_ref=buf.at[slot + own, chunk(i)],
            send_sem=ssem.at[number, i],
            recv_sem=rsem.at[slot + own, i],
            device_id={"scan": at(offset)},
        )

    def arrive(slot, i):
        pltpu.make_async_copy(
            tile_ref.at[chunk(i)], buf.at[slot + own, chunk(i)], rsem.at[slot + own, i]
        ).wait()

    @pl.loop(0, chunks)
    def _(i):
        send(x_own, i).start()
        send(z_own, i).start()
        send(core_own, i).start()

    load_tile.wait()

    def column_stats(ref, pieces):
        size = pixels // pieces
        width = ref.shape[-1]

        def piece(i):
            return ref[pl.ds(pl.multiple_of(i * size, 16), size), :].astype(jnp.float32)

        zero = jnp.zeros((1, width), jnp.float32)
        mean = lax.fori_loop(
            0, pieces, lambda i, s: s + jnp.sum(piece(i), axis=0, keepdims=True), zero
        ) / pixels

        def squares(i, s):
            c = piece(i) - mean
            return s + jnp.sum(c * c, axis=0, keepdims=True)

        mean_square = lax.fori_loop(0, pieces, squares, zero) / pixels
        return mean, lax.rsqrt((mean_square + EPS) * pixels)

    mean, scale = column_stats(buf.at[own], 15)
    live = (
        lax.broadcasted_iota(jnp.int32, (1, slots), 1) < valid_ref[0]
    ).astype(jnp.float32)
    phase = phase_ref[...]
    meta[own, 0:4, :] = quats_ref[...].astype(jnp.float32) * live
    for p in range(3):
        meta[own, 4 + p : 5 + p, :] = (phase == p).astype(jnp.float32) * live
    meta[own, 7:8, :] = live
    meta[own, 8:9, :] = mean
    meta[own, 9:10, :] = scale
    meta[own, 10:16, :] = jnp.zeros((6, slots), jnp.float32)

    def send_meta(index, offset):
        there = jnp.where(lax.rem(at(offset), LAYER) < 2, 1, -1)
        slot = own - there * offset
        return pltpu.make_async_remote_copy(
            src_ref=meta.at[own],
            dst_ref=meta.at[slot],
            send_sem=meta_ssem.at[index],
            recv_sem=meta_rsem.at[slot],
            device_id={"scan": at(offset)},
        )

    offsets = (-3, -2, -1, 1, 2, 3)
    for index, offset in enumerate(offsets):
        send_meta(index, offset).start()

    load_pats.wait()
    p_mean, p_scale = column_stats(pats, 25)

    @pl.loop(0, 25)
    def _(i):
        part = pl.ds(pl.multiple_of(i * (pixels // 25), 16), pixels // 25)
        pats[part, :] = ((pats[part, :].astype(jnp.float32) - p_mean) * p_scale).astype(
            jnp.bfloat16
        )

    totals[...] = jnp.zeros_like(totals)

    def meta_arrive(slot):
        pltpu.make_async_copy(
            meta.at[own], meta.at[slot + own], meta_rsem.at[slot + own]
        ).wait()

    def accumulate(which, slot, i):
        m = meta[slot + own, 8:9, :]
        s = meta[slot + own, 9:10, :]
        unit = ((buf[slot + own, chunk(i), :].astype(jnp.float32) - m) * s).astype(
            jnp.bfloat16
        )
        product = lax.dot_general(
            unit, pats[chunk(i), :], (((0,), (0,)), ((), ())),
            preferred_element_type=jnp.float32,
        )

        @pl.when(i == 0)
        def _():
            acc[which] = product

        @pl.when(i > 0)
        def _():
            acc[which] += product

    def finish(which, slot):
        weights = jnp.exp(SHARPNESS * (acc[which] - 1.0)).astype(jnp.bfloat16)
        table = meta[slot + own, 0:8, :].astype(jnp.bfloat16)
        totals[...] += jnp.dot(table, weights, preferred_element_type=jnp.float32)

    meta_arrive(rho)

    @pl.loop(0, chunks)
    def _(i):
        arrive(rho, i)
        accumulate(0, 0, i)
        accumulate(1, rho, i)

    finish(0, 0)
    finish(1, rho)

    z_slot = -3 * rho
    meta_arrive(2)
    meta_arrive(z_slot)

    @pl.loop(0, chunks)
    def _(i):
        arrive(2, i)
        arrive(z_slot, i)
        send(relay, i).start()
        send(core_mid, i).start()
        accumulate(0, 2, i)
        accumulate(1, z_slot, i)

    finish(0, 2)
    finish(1, z_slot)

    mid_slot = 2 + rho
    meta_arrive(mid_slot)

    @pl.loop(0, chunks)
    def _(i):
        arrive(mid_slot, i)
        accumulate(0, mid_slot, i)

    finish(0, mid_slot)

    far_slot = -2 - role
    near_slot = -1 - role
    meta_arrive(far_slot)
    meta_arrive(near_slot)

    @pl.loop(0, chunks)
    def _(i):
        arrive(far_slot, i)

        @pl.when(role == 0)
        def _():
            send(core_far, i).start()

        arrive(near_slot, i)

        @pl.when(role == 0)
        def _():
            send(core_near, i).start()

        accumulate(0, far_slot, i)
        accumulate(1, near_slot, i)

    finish(0, far_slot)
    finish(1, near_slot)

    sums[my_dict] = totals[...]

    def send_sum(d):
        return pltpu.make_async_remote_copy(
            src_ref=totals,
            dst_ref=sums.at[my_dict],
            send_sem=sum_ssem.at[d],
            recv_sem=sum_rsem.at[my_dict],
            device_id={"dict": lax.rem(my_dict + d, n_dict)},
        )

    for d in range(1, n_dict):
        send_sum(d).start()
    for d in range(1, n_dict):
        source = lax.rem(my_dict + d, n_dict)
        pltpu.make_async_copy(totals, sums.at[source], sum_rsem.at[source]).wait()
    whole = sums[0]
    for d in range(1, n_dict):
        whole = whole + sums[d]
    denominator = whole[7:8]
    quat_out[...] = whole[0:4] / denominator
    prob_out[...] = whole[4:7] / denominator

    @pl.loop(0, chunks)
    def _(i):
        for flow in (x_own, z_own, core_own, relay, core_mid):
            send(flow, i).wait_send()

        @pl.when(role == 0)
        def _():
            send(core_far, i).wait_send()
            send(core_near, i).wait_send()

    for index, offset in enumerate(offsets):
        send_meta(index, offset).wait_send()
    for d in range(1, n_dict):
        send_sum(d).wait_send()


def solution(mesh):
    n = mesh.shape["scan"]
    n_dict = mesh.shape["dict"]

    def per_device(patterns, dictionary, orientation_quats, phase_id, valid_count):
        pixels, slots = dictionary.shape
        count = patterns.shape[1]
        chunks = chunk_count(pixels)
        vmem = pl.BlockSpec(memory_space=pltpu.VMEM)
        hbm = pl.BlockSpec(memory_space=pltpu.HBM)
        return pl.pallas_call(
            functools.partial(kernel, n, n_dict, chunks),
            out_shape=(
                jax.ShapeDtypeStruct((4, count), jnp.float32),
                jax.ShapeDtypeStruct((3, count), jnp.float32),
            ),
            in_specs=[hbm, hbm, vmem, vmem, pl.BlockSpec(memory_space=pltpu.SMEM)],
            out_specs=(vmem, vmem),
            scratch_shapes=[
                pltpu.VMEM((SLOTS, pixels, slots), jnp.bfloat16),
                pltpu.VMEM((pixels, count), jnp.bfloat16),
                pltpu.VMEM((SLOTS, 16, slots), jnp.float32),
                pltpu.VMEM((2, slots, count), jnp.float32),
                pltpu.VMEM((n_dict, 8, count), jnp.float32),
                pltpu.VMEM((8, count), jnp.float32),
                pltpu.SemaphoreType.DMA((7, chunks)),
                pltpu.SemaphoreType.DMA((SLOTS, chunks)),
                pltpu.SemaphoreType.DMA((6,)),
                pltpu.SemaphoreType.DMA((SLOTS,)),
                pltpu.SemaphoreType.DMA((2,)),
                pltpu.SemaphoreType.DMA((n_dict,)),
                pltpu.SemaphoreType.DMA((n_dict,)),
            ],
            compiler_params=pltpu.CompilerParams(
                collective_id=0, has_side_effects=True, vmem_limit_bytes=48 * 2**20
            ),
        )(dictionary, patterns, orientation_quats, phase_id.reshape(1, slots), valid_count)

    in_specs = (
        P(None, "scan"),
        P(None, ("scan", "dict")),
        P(None, ("scan", "dict")),
        P(("scan", "dict")),
        P(("scan", "dict")),
    )
    out_specs = (P(None, "scan"), P(None, "scan"))
    return jax.shard_map(
        per_device, mesh=mesh, in_specs=in_specs, out_specs=out_specs, check_vma=False
    )
```

time: 157 us -> 83 us (0.53)
  waiting for transfers between devices: 88.4 us -> 0 us
  Pallas kernels: 0 us -> 77.5 us
  matrix products: 41.7 us -> 0 us
  other arithmetic: 11.1 us -> 0 us
  starting transfers between devices: 7.79 us -> 0 us
  blocking collectives: 6.35 us -> 0 us
  local copies, waits for them, and re-layouts: 0.1 us -> 4.07 us
    ppermute x6 -> x0, waiting for transfers between devices: 88.4 us -> none  [from_behind(): return lax.ppermute(block, axis, route)]
    pallas_call x0 -> x1, Pallas kernels: none -> 77.5 us  [per_device(): pl.pallas_call(functools.partial(kernel, n, n_dict, chunks), out_shape=(j...]
    dot_general x7 -> x0, matrix products: 41.7 us -> none  [contribute(): return jnp.dot(table_rows, weights, preferred_element_type=jnp.float32)]
    ppermute x6 -> x0, starting transfers between devices: 7.79 us -> none  [from_behind(): return lax.ppermute(block, axis, route)]
    reduce_sum x4 -> x0, other arithmetic: 7.71 us -> none  [the longest x2 4.47 us: unit_columns(): mean_square = jnp.mean(centred * centred, axis=0, keepdims=True)]
    psum x1 -> x0, blocking collectives: 6.35 us -> none  [per_device(): totals = lax.psum(running, 'dict')]
    unnamed x6 -> x8, local copies, waits for them, and re-layouts: 0.01 us -> 4.07 us
    convert_element_type x5 -> x0, other arithmetic: 2.04 us -> none  [the longest x1 1.95 us: unit_columns(): (centred * lax.rsqrt((mean_square + EPS) * values.shape[0])).astype(jnp.b...]
  transfers between devices with their start and end apart: 6 -> 0, of which waited for: 5 -> 0; matrix products, arithmetic and copies ran while one was open for 25% -> 0% of each run, Pallas kernels for 0% -> 0%
where the time goes in v1:
time: 83 us; the launch traced here: 82.8 us
  Pallas kernels  77.5 us (93%)
  local copies, waits for them, and re-layouts  4.07 us (5%)
  between operations  1.3 us (2%)
    pallas_call x1, Pallas kernels, per_device(): pl.pallas_call(functools.partial(kernel, n, n_dict, chunks), out_shape=(j...  77.5 us
    unnamed x8, local copies, waits for them, and re-layouts  4.07 us

profile of v1, /device:TPU:1, one launch (start us, length us, event | category | flops | bytes accessed | tf_op | source)
XLA Modules:
  0.0 82.8 jit_solution(8449785010154936582)
XLA Ops:
  1.3 0.0 copy-start
  1.3 1.5 %copy-done = bf16[3600,256]{1,0:T(8,128)(2,1)S(1)} copy-done((bf16[3600,256]{1,0:T(8,128)(2,1)S(1)}, bf16[3600,256]{1,0:T(8,128)(2,1)}, u32[]{:S(2)}) %copy-start) | copy-done | bytes 1843224
  2.8 0.0 copy-start.1
  2.8 0.7 copy-done.1
  3.5 0.0 copy-start.2
  3.5 0.7 copy-done.2
  4.1 77.5 %shard_map.68 = (f32[4,1024]{1,0:T(4,128)S(1)}, f32[3,1024]{1,0:T(4,128)S(1)}) custom-call(bf16[3600,256]{1,0:T(8,128)(2,1)S(1)} %copy-done, bf16[3600,1024]{1,0:T(8,128)(2,1)} %pats_ref.1, bf16[4,256]{1,0:T(4,128)(2,1)S(1)} %copy-done.1, s32[1,256]{1,0:T(1,128)S(1)} %bitcast.1, s32[1]{0:T(128)S(6)} %copy.9.valid_ref), custom_call_target="tpu_custom_call" | custom-call | tf_op jit(solution)/shard_map/pallas_call | solution.py:291
  81.6 0.6 copy.10
  82.2 0.6 copy.11
Async XLA Ops:
  1.3 1.5 %copy-start = (bf16[3600,256]{1,0:T(8,128)(2,1)S(1)}, bf16[3600,256]{1,0:T(8,128)(2,1)}, u32[]{:S(2)}) copy-start(bf16[3600,256]{1,0:T(8,128)(2,1)} %tile_ref.1) | copy-start | bytes 5529604
  2.8 0.7 copy-start.1
  3.5 0.7 copy-start.2

commit v2 on v1

--- a/solution.py
+++ b/solution.py
@@ -189,8 +189,6 @@
     finish(1, rho)
 
     z_slot = -3 * rho
-    meta_arrive(2)
-    meta_arrive(z_slot)
 
     @pl.loop(0, chunks)
     def _(i):
@@ -198,6 +196,12 @@
         arrive(z_slot, i)
         send(relay, i).start()
         send(core_mid, i).start()
+
+    meta_arrive(2)
+    meta_arrive(z_slot)
+
+    @pl.loop(0, chunks)
+    def _(i):
         accumulate(0, 2, i)
         accumulate(1, z_slot, i)
 

time: 83 us -> 87.6 us (1.055)
  the two profiles are of different devices: /device:TPU:1 before, /device:TPU:2 now
where the time goes in v2:
time: 87.6 us; the launch traced here: 87.4 us
  Pallas kernels  82 us (94%)
  local copies, waits for them, and re-layouts  4.07 us (5%)
  between operations  1.3 us (1%)
    pallas_call x1, Pallas kernels, per_device(): pl.pallas_call(functools.partial(kernel, n, n_dict, chunks), out_shape=(j...  82 us
    unnamed x8, local copies, waits for them, and re-layouts  4.07 us

profile of v2, /device:TPU:2, one launch (start us, length us, event | category | flops | bytes accessed | tf_op | source)
XLA Modules:
  0.0 87.4 jit_solution(10672944406080871065)
XLA Ops:
  1.3 0.0 copy-start
  1.3 1.5 %copy-done = bf16[3600,256]{1,0:T(8,128)(2,1)S(1)} copy-done((bf16[3600,256]{1,0:T(8,128)(2,1)S(1)}, bf16[3600,256]{1,0:T(8,128)(2,1)}, u32[]{:S(2)}) %copy-start) | copy-done | bytes 1843224
  2.8 0.0 copy-start.1
  2.8 0.7 copy-done.1
  3.5 0.0 copy-start.2
  3.5 0.7 copy-done.2
  4.1 82.0 %shard_map.68 = (f32[4,1024]{1,0:T(4,128)S(1)}, f32[3,1024]{1,0:T(4,128)S(1)}) custom-call(bf16[3600,256]{1,0:T(8,128)(2,1)S(1)} %copy-done, bf16[3600,1024]{1,0:T(8,128)(2,1)} %pats_ref.1, bf16[4,256]{1,0:T(4,128)(2,1)S(1)} %copy-done.1, s32[1,256]{1,0:T(1,128)S(1)} %bitcast.1, s32[1]{0:T(128)S(6)} %copy.9.valid_ref), custom_call_target="tpu_custom_call" | custom-call | tf_op jit(solution)/shard_map/pallas_call | solution.py:295
  86.2 0.6 copy.10
  86.8 0.6 copy.11
Async XLA Ops:
  1.3 1.5 %copy-start = (bf16[3600,256]{1,0:T(8,128)(2,1)S(1)}, bf16[3600,256]{1,0:T(8,128)(2,1)}, u32[]{:S(2)}) copy-start(bf16[3600,256]{1,0:T(8,128)(2,1)} %tile_ref.1) | copy-start | bytes 5529604
  2.8 0.7 copy-start.1
  3.5 0.7 copy-start.2
